TPU v7x, 1024 devices: a whole 8x8x8 slice. The times are simulated.
1024 devices in a mesh: seq: 64 (over z, y), tp: 16 (over x, core).
Axes of the slice: x: 8, y: 8, z: 8, core: 2. Of those that a mesh axis runs over, the one named last changes fastest.
Arguments:
- queries: bfloat16 [8192, 2048], P('seq', 'tp'), may hold values from -4.5 to 4.5
- keys: bfloat16 [8192, 2048], P('seq', 'tp'), may hold values from -4.5 to 4.5
- values: bfloat16 [8192, 2048], P('seq', 'tp'), may hold values from -6 to 6
- step_rate: float32 [16], P('tp'), may hold values from 0.00390625 to 0.125
- memory_init: float32 [16, 128, 128], P('tp'), may hold values from -0.5 to 0.5
- out_weight: bfloat16 [2048, 2048], P('tp'), may hold values from -0.125 to 0.125
Outputs:
- layer_out: bfloat16 [8192, 2048], P('seq', 'tp')
All inputs are finite; a program needn't handle non-finite values.
Results may differ from a plain program's by a relative error of at most 0.018.
Values may be sent and summed in bfloat16 or wider, within the bound.
A program may use at most 32 MiB of HBM per device.

v0:
```python
import math

import jax
import jax.numpy as jnp
from jax import lax
from jax.sharding import PartitionSpec as P

WIN = 1024
CH = 16


highest = lax.Precision.HIGHEST


def prefix(shard, axis, combine, identity):
    size, position = (lax.axis_size(axis), lax.axis_index(axis))
    everything = jax.tree.map(lambda part: lax.all_gather(part, axis), shard)
    start = jax.tree.map(
        lambda part, zero: jnp.broadcast_to(jnp.asarray(zero, part.dtype), part.shape),
        shard,
        identity,
    )

    def hop(k, before):
        reached = k < position
        new = combine(before, jax.tree.map(lambda part: part[k], everything))
        return jax.tree.map(lambda a, b: jnp.where(reached, a, b), new, before)

    return lax.fori_loop(0, size, hop, start)


def shifted(block, axis, distance):
    devices = range(lax.axis_size(axis))
    route = [(i - distance, i) for i in devices if i - distance in devices]
    return lax.ppermute(block, axis, route)


def unit_keys(keys_float, head_size):
    mean_square = jnp.mean(keys_float * keys_float, axis=-1, keepdims=True)
    return keys_float / jnp.sqrt(head_size * (mean_square + 1e-06))


def compose(earlier, later):
    linear_part = jnp.einsum("...ij,...jk->...ik", later[0], earlier[0], precision=highest)
    offset_part = (
        jnp.einsum("...ij,...jk->...ik", later[0], earlier[1], precision=highest) + later[1]
    )
    return (linear_part, offset_part)


def shards(queries, keys, values, step_rate, memory_init, out_weight):
    tok_rows = queries.shape[0]
    head_count = memory_init.shape[0]
    head_size = memory_init.shape[1]
    q_heads = queries.reshape(tok_rows, head_count, head_size)
    k_heads = keys.reshape(tok_rows, head_count, head_size)
    group_count = tok_rows // CH
    key_blocks = unit_keys(k_heads.astype(jnp.float32), head_size).reshape(
        group_count, CH, head_count, head_size
    )
    value_blocks = values.astype(jnp.float32).reshape(group_count, CH, head_count, head_size)
    query_blocks = queries.astype(jnp.float32).reshape(group_count, CH, head_count, head_size)
    gram = jnp.einsum("cthi,cthj->chij", key_blocks, key_blocks, precision=highest)
    cross = jnp.einsum("cthi,cthj->chij", key_blocks, value_blocks, precision=highest)
    rates = step_rate[None, :, None, None]
    identity_mat = jnp.broadcast_to(
        jnp.eye(head_size, dtype=jnp.float32), (head_count, head_size, head_size)
    )
    zero_mat = jnp.zeros((head_count, head_size, head_size), jnp.float32)
    shrink = identity_mat[None] - rates * gram
    inject = rates * cross
    prefix_lin, prefix_off = lax.associative_scan(compose, (shrink, inject), axis=0)
    before_lin, before_off = prefix(
        (prefix_lin[-1], prefix_off[-1]), "seq", compose, (identity_mat, zero_mat)
    )
    device_state = (
        jnp.einsum("hij,hjk->hik", before_lin, memory_init, precision=highest) + before_off
    )
    group_lin = jnp.concatenate([identity_mat[None], prefix_lin[:-1]], axis=0)
    group_off = jnp.concatenate([zero_mat[None], prefix_off[:-1]], axis=0)
    states = jnp.einsum("chij,hjk->chik", group_lin, device_state, precision=highest) + group_off
    memory_read = jnp.einsum("cthi,chij->cthj", query_blocks, states, precision=highest).reshape(
        tok_rows, head_count, head_size
    )
    reach = -(-WIN // tok_rows)
    kv_pair = jnp.stack([keys, values])
    earlier_pieces = []
    moving = kv_pair
    for distance in range(reach):
        moving = shifted(moving, "seq", 1)
        earlier_pieces.insert(0, moving)
    buffer = jnp.concatenate(earlier_pieces + [kv_pair], axis=1)
    device_index = lax.axis_index("seq")
    query_block = math.gcd(512, tok_rows)
    block_count = tok_rows // query_block
    span_len = WIN + query_block

    def attend(block_index):
        offset = block_index * query_block
        key_part = buffer[0].reshape(span_len, head_count, head_size)
        value_part = buffer[1].reshape(span_len, head_count, head_size)
        query_pos = device_index * tok_rows + offset + jnp.arange(query_block, dtype=jnp.int32)
        key_pos = device_index * tok_rows + offset - WIN + jnp.arange(span_len, dtype=jnp.int32)
        allowed = (
            (key_pos[None, :] <= query_pos[:, None])
            & (key_pos[None, :] > query_pos[:, None] - WIN)
            & (key_pos[None, :] >= 0)
        )
        scores = jnp.einsum(
            "qhd,khd->hqk", q_heads, key_part, preferred_element_type=jnp.float32
        ) * (1.0 / math.sqrt(head_size))
        scores = jnp.where(allowed[None], scores, -jnp.inf)
        maxima = jnp.max(scores, axis=-1, keepdims=True)
        expd = jnp.where(allowed[None], jnp.exp(scores - maxima), 0.0)
        totals = jnp.sum(expd, axis=-1, keepdims=True)
        probs = (expd / totals).astype(jnp.bfloat16)
        return jnp.einsum("hqk,khd->qhd", probs, value_part, preferred_element_type=jnp.float32)

    attended = lax.map(attend, jnp.arange(block_count, dtype=jnp.int32)).reshape(
        tok_rows, head_count, head_size
    )
    gated = (
        (attended * jax.nn.sigmoid(memory_read))
        .astype(jnp.bfloat16)
        .reshape(tok_rows, head_count * head_size)
    )
    summed = lax.psum_scatter(
        lax.dot_general(
            out_weight, gated, (((0,), (1,)), ((), ())), preferred_element_type=jnp.float32
        ).astype(jnp.bfloat16),
        "tp",
        scatter_dimension=0,
        tiled=True,
    ).astype(jnp.float32)
    return jnp.transpose(summed).astype(jnp.bfloat16)


def solution(mesh):
    return jax.shard_map(
        shards,
        mesh=mesh,
        in_specs=(
            P("seq", "tp"),
            P("seq", "tp"),
            P("seq", "tp"),
            P("tp"),
            P("tp", None, None),
            P("tp", None),
        ),
        out_specs=P("seq", "tp"),
        check_vma=False,
    )
```

profile of v0, /device:TPU:1, one launch (start us, length us, event | category | flops | bytes accessed | tf_op | source)
XLA Modules:
  0.0 425.3 jit_solution(14181487117020122316)
XLA Ops:
  10.7 1.4 convolution_multiply_fusion.1
  16.5 4.2 collective-permute-start
  20.7 1.2 collective-permute-done
  22.0 3.7 collective-permute-start.1
  25.8 1.2 collective-permute-done.1
  27.0 3.7 collective-permute-start.2
  30.7 1.2 collective-permute-done.2
  32.0 3.8 collective-permute-start.3
  35.7 1.3 collective-permute-done.3
  37.0 4.9 %collective-permute-start.4 = (bf16[2,128,128]{2,1,0:T(8,128)(2,1)S(1)}, bf16[2,128,128]{2,1,0:T(8,128)(2,1)S(1)}, u32[]{:S(2)}, u32[]{:S(2)}) collective-permute-start(bf16[2,128,128]{2,1,0:T(8,128)(2,1)S(1)} %collective-permute-done.3), channel_id=1, source_target_pairs={{0,16},{16,32},{32,48},{48,64},{64,80},{80,96},{96,112},{112,128},... | collective-permute-start | bytes 196616 | tf_op jit(solution)/shard_map/ppermute | solution.py:35
  42.0 1.3 collective-permute-done.4
  43.2 4.9 %collective-permute-start.5 = (bf16[2,128,128]{2,1,0:T(8,128)(2,1)S(1)}, bf16[2,128,128]{2,1,0:T(8,128)(2,1)S(1)}, u32[]{:S(2)}, u32[]{:S(2)}) collective-permute-start(bf16[2,128,128]{2,1,0:T(8,128)(2,1)S(1)} %collective-permute-done.4), channel_id=1, source_target_pairs={{0,16},{16,32},{32,48},{48,64},{64,80},{80,96},{96,112},{112,128},... | collective-permute-start | bytes 196616 | tf_op jit(solution)/shard_map/ppermute | solution.py:35
  48.2 1.3 collective-permute-done.5
  49.5 4.9 %collective-permute-start.6 = (bf16[2,128,128]{2,1,0:T(8,128)(2,1)S(1)}, bf16[2,128,128]{2,1,0:T(8,128)(2,1)S(1)}, u32[]{:S(2)}, u32[]{:S(2)}) collective-permute-start(bf16[2,128,128]{2,1,0:T(8,128)(2,1)S(1)} %collective-permute-done.5), channel_id=1, source_target_pairs={{0,16},{16,32},{32,48},{48,64},{64,80},{80,96},{96,112},{112,128},... | collective-permute-start | bytes 196616 | tf_op jit(solution)/shard_map/ppermute | solution.py:35
  54.4 1.3 collective-permute-done.6
  55.7 4.9 %collective-permute-start.7 = (bf16[2,128,128]{2,1,0:T(8,128)(2,1)S(1)}, bf16[2,128,128]{2,1,0:T(8,128)(2,1)S(1)}, u32[]{:S(2)}, u32[]{:S(2)}) collective-permute-start(bf16[2,128,128]{2,1,0:T(8,128)(2,1)S(1)} %collective-permute-done.6), channel_id=1, source_target_pairs={{0,16},{16,32},{32,48},{48,64},{64,80},{80,96},{96,112},{112,128},... | collective-permute-start | bytes 196616 | tf_op jit(solution)/shard_map/ppermute | solution.py:35
  60.6 1.5 collective-permute-done.7
  63.5 54.1 %all-gather.5.cloned.1.call-done = f32[64,1,128,128]{3,2,1,0:T(8,128)} async-done(((f32[1,1,128,128]{3,2,1,0:T(8,128)}), f32[64,1,128,128]{3,2,1,0:T(8,128)}) %all-gather.5.cloned.1.call-update) | async-done | bytes 4194320 | tf_op jit(solution)/shard_map/all_gather | solution.py:17
  117.6 94.8 %all-gather.3.cloned.1.call-done = f32[64,1,128,128]{3,2,1,0:T(8,128)} async-done(((f32[1,1,128,128]{3,2,1,0:T(8,128)}), f32[64,1,128,128]{3,2,1,0:T(8,128)}) %all-gather.3.cloned.1.call-update) | async-done | bytes 4194320 | tf_op jit(solution)/shard_map/all_gather | solution.py:17
  212.4 140.6 %while.20 = (s32[]{:T(128)}, f32[1,128,128]{2,1,0:T(8,128)S(1)}, f32[1,128,128]{2,1,0:T(8,128)S(1)}, s32[]{:T(128)}, f32[64,1,128,128]{3,2,1,0:T(8,128)}, /*index=5*/f32[64,1,128,128]{3,2,1,0:T(8,128)}, s32[]{:T(128)}, s32[]{:T(128)}) while((s32[]{:T(128)}, f32[1,128,128]{2,1,0:T(8,128)S(1)}, f32[1,128,128]{2,1,0:T(8,128)S(1)}, ...), condition=%wide.region_4.5_spmd.clone, body=%wide.region_3.4_spmd.clone.sunk | while | flops 50413572 | bytes 854644 | solution.py:29
  216.8 1.1 fusion.111
  219.0 1.1 fusion.111
  356.2 61.0 %reduce-scatter.4.cloned.1.call-done = bf16[128,128]{1,0:T(8,128)(2,1)} async-done(((bf16[2048,128]{1,0:T(8,128)(2,1)}), bf16[128,128]{1,0:T(8,128)(2,1)}) %reduce-scatter.4.cloned.1.call-update) | async-done | bytes 32784
  417.3 1.5 copy.23
  (337 shorter events, 147.4 us)
Async XLA Ops:
  6.5 347.8 %copy-start = (bf16[128,2048]{1,0:T(8,128)(2,1)S(1)}, bf16[128,2048]{1,0:T(8,128)(2,1)}, u32[]{:S(2)}) copy-start(bf16[128,2048]{1,0:T(8,128)(2,1)} %param.13) | copy-start | bytes 1572868
  6.5 111.1 %all-gather.5.cloned.1.call-start = ((), (), s32[]{:S(2)}) async-start(), calls=%async_computation.2 | async-start | bytes 4259840 | tf_op jit(solution)/shard_map/all_gather | solution.py:17
  13.7 2.8 copy-start.1
  13.7 2.8 copy-start.2
  14.5 197.8 %all-gather.3.cloned.1.call-start = ((), (), s32[]{:S(2)}) async-start(), calls=%async_computation.1 | async-start | bytes 4259840 | tf_op jit(solution)/shard_map/all_gather | solution.py:17
  15.3 47.0 %copy-start.4 = (bf16[128,128]{1,0:T(8,128)(2,1)S(1)}, bf16[128,128]{1,0:T(8,128)(2,1)}, u32[]{:S(2)}) copy-start(bf16[128,128]{1,0:T(8,128)(2,1)} %param.8) | copy-start | bytes 98308
  16.4 400.9 %reduce-scatter.4.cloned.1.call-start = ((), (), s32[]{:S(2)}) async-start(), calls=%async_computation.3 | async-start | bytes 557056
  16.5 5.5 %collective-permute-start = (bf16[2,128,128]{2,1,0:T(8,128)(2,1)S(1)}, bf16[2,128,128]{2,1,0:T(8,128)(2,1)S(1)}, u32[]{:S(2)}, u32[]{:S(2)}) collective-permute-start(bf16[2,128,128]{2,1,0:T(8,128)(2,1)S(1)} %pad_maximum_fusion.4), channel_id=1, source_target_pairs={{0,16},{16,32},{32,48},{48,64},{64,80},{80,96},{96,112},{112,128},... | collective-permute-start | bytes 196616 | tf_op jit(solution)/shard_map/ppermute | solution.py:35
  22.0 5.0 %collective-permute-start.1 = (bf16[2,128,128]{2,1,0:T(8,128)(2,1)S(1)}, bf16[2,128,128]{2,1,0:T(8,128)(2,1)S(1)}, u32[]{:S(2)}, u32[]{:S(2)}) collective-permute-start(bf16[2,128,128]{2,1,0:T(8,128)(2,1)S(1)} %collective-permute-done), channel_id=1, source_target_pairs={{0,16},{16,32},{32,48},{48,64},{64,80},{80,96},{96,112},{112,128},... | collective-permute-start | bytes 196616 | tf_op jit(solution)/shard_map/ppermute | solution.py:35
  25.8 327.3 %copy-start.3 = (f32[1,128,128]{2,1,0:T(8,128)S(1)}, f32[1,128,128]{2,1,0:T(8,128)}, u32[]{:S(2)}) copy-start(f32[1,128,128]{2,1,0:T(8,128)} %param.12) | copy-start | bytes 196612
  27.0 5.0 %collective-permute-start.2 = (bf16[2,128,128]{2,1,0:T(8,128)(2,1)S(1)}, bf16[2,128,128]{2,1,0:T(8,128)(2,1)S(1)}, u32[]{:S(2)}, u32[]{:S(2)}) collective-permute-start(bf16[2,128,128]{2,1,0:T(8,128)(2,1)S(1)} %collective-permute-done.1), channel_id=1, source_target_pairs={{0,16},{16,32},{32,48},{48,64},{64,80},{80,96},{96,112},{112,128},... | collective-permute-start | bytes 196616 | tf_op jit(solution)/shard_map/ppermute | solution.py:35
  32.0 5.1 %collective-permute-start.3 = (bf16[2,128,128]{2,1,0:T(8,128)(2,1)S(1)}, bf16[2,128,128]{2,1,0:T(8,128)(2,1)S(1)}, u32[]{:S(2)}, u32[]{:S(2)}) collective-permute-start(bf16[2,128,128]{2,1,0:T(8,128)(2,1)S(1)} %collective-permute-done.2), channel_id=1, source_target_pairs={{0,16},{16,32},{32,48},{48,64},{64,80},{80,96},{96,112},{112,128},... | collective-permute-start | bytes 196616 | tf_op jit(solution)/shard_map/ppermute | solution.py:35
  37.0 6.2 %collective-permute-start.4 = (bf16[2,128,128]{2,1,0:T(8,128)(2,1)S(1)}, bf16[2,128,128]{2,1,0:T(8,128)(2,1)S(1)}, u32[]{:S(2)}, u32[]{:S(2)}) collective-permute-start(bf16[2,128,128]{2,1,0:T(8,128)(2,1)S(1)} %collective-permute-done.3), channel_id=1, source_target_pairs={{0,16},{16,32},{32,48},{48,64},{64,80},{80,96},{96,112},{112,128},... | collective-permute-start | bytes 196616 | tf_op jit(solution)/shard_map/ppermute | solution.py:35
  43.2 6.2 %collective-permute-start.5 = (bf16[2,128,128]{2,1,0:T(8,128)(2,1)S(1)}, bf16[2,128,128]{2,1,0:T(8,128)(2,1)S(1)}, u32[]{:S(2)}, u32[]{:S(2)}) collective-permute-start(bf16[2,128,128]{2,1,0:T(8,128)(2,1)S(1)} %collective-permute-done.4), channel_id=1, source_target_pairs={{0,16},{16,32},{32,48},{48,64},{64,80},{80,96},{96,112},{112,128},... | collective-permute-start | bytes 196616 | tf_op jit(solution)/shard_map/ppermute | solution.py:35
  49.5 6.3 %collective-permute-start.6 = (bf16[2,128,128]{2,1,0:T(8,128)(2,1)S(1)}, bf16[2,128,128]{2,1,0:T(8,128)(2,1)S(1)}, u32[]{:S(2)}, u32[]{:S(2)}) collective-permute-start(bf16[2,128,128]{2,1,0:T(8,128)(2,1)S(1)} %collective-permute-done.5), channel_id=1, source_target_pairs={{0,16},{16,32},{32,48},{48,64},{64,80},{80,96},{96,112},{112,128},... | collective-permute-start | bytes 196616 | tf_op jit(solution)/shard_map/ppermute | solution.py:35
  55.7 6.4 %collective-permute-start.7 = (bf16[2,128,128]{2,1,0:T(8,128)(2,1)S(1)}, bf16[2,128,128]{2,1,0:T(8,128)(2,1)S(1)}, u32[]{:S(2)}, u32[]{:S(2)}) collective-permute-start(bf16[2,128,128]{2,1,0:T(8,128)(2,1)S(1)} %collective-permute-done.6), channel_id=1, source_target_pairs={{0,16},{16,32},{32,48},{48,64},{64,80},{80,96},{96,112},{112,128},... | collective-permute-start | bytes 196616 | tf_op jit(solution)/shard_map/ppermute | solution.py:35
Sparse Core Ops, SparseCore 0:
  14.7 102.8 all-gather.4
  121.8 90.5 all-gather.2
  356.4 60.8 reduce-scatter.3
where the time goes:
time: 432 us; the launch traced here: 425 us
  waiting for transfers between devices  220 us (51%)
  matrix products  144 us (33%)
  starting transfers between devices  35 us (8%)
  between operations  14.4 us (3%)
    all_gather x2, waiting for transfers between devices, prefix(): everything = jax.tree.map(lambda part: lax.all_gather(part, axis), shard)  149 us
    dot_general x69, matrix products, compose(): jnp.einsum('...ij,...jk->...ik', later[0], earlier[1], precision=highest)  70.7 us
    dot_general x69, matrix products, compose(): jnp.einsum('...ij,...jk->...ik', later[0], earlier[0], precision=highest)  68.5 us
    unnamed x4, waiting for transfers between devices  61.1 us
    ppermute x8, starting transfers between devices, shifted(): return lax.ppermute(block, axis, route)  34.9 us
    ppermute x8, waiting for transfers between devices, shifted(): return lax.ppermute(block, axis, route)  10.3 us
  transfers between devices with their start and end apart: 11, of which 11 were waited for; matrix products, arithmetic and copies ran while one was open for 1% of the time, Pallas kernels for 0%

commit v1 on v0

v1 whole, which is shorter than its diff:
```python
import functools
import math

import jax
import jax.numpy as jnp
from jax import lax
from jax.experimental import pallas as pl
from jax.experimental.pallas import tpu as pltpu
from jax.sharding import PartitionSpec as P

WIN = 1024
CH = 16
MESH = pl.DeviceIdType.MESH
F32 = jnp.float32
BF16 = jnp.bfloat16


def mm(a, b):
    return lax.dot_general(a, b, (((1,), (0,)), ((), ())), preferred_element_type=F32)


def mm_bt(a, b):
    return lax.dot_general(a, b, (((1,), (1,)), ((), ())), preferred_element_type=F32)


def mm_at(a, b):
    return lax.dot_general(a, b, (((0,), (0,)), ((), ())), preferred_element_type=F32)


def kernel(
    S, T, W,
    rate_ref, q_ref, k_ref, v_ref, init_ref, w_ref, o_ref,
    kbuf, vbuf, zbuf, gbuf, wbuf,
    kv_send, kv_recv, z_send, z_recv, g_send, g_recv, w_send, w_recv,
):
    n, hd = q_ref.shape
    X = T // 2
    NZ = S // W
    up, zup = W // 2, NZ // 2
    s, t = lax.axis_index("seq"), lax.axis_index("tp")
    x, core, z = t // 2, lax.rem(t, 2), s // W
    s_next, s_prev = lax.rem(s + 1, S), lax.rem(s + S - 1, S)
    z_next, z_prev = lax.rem(s + W, S), lax.rem(s + S - W, S)
    partner = x * 2 + 1 - core

    def peer(j, other):
        xj = lax.rem(x + j, X)
        return xj * 2 + (1 - core if other else core)

    barrier = pltpu.get_barrier_semaphore()
    near = (s_next, s_prev, z_next, z_prev)
    for dev in near:
        pl.semaphore_signal(barrier, inc=1, device_id=(dev, t), device_id_type=MESH)
    for j in range(X):
        for other in (0, 1):
            if j or other:
                pl.semaphore_signal(
                    barrier, inc=1, device_id=(s, peer(j, other)), device_id_type=MESH
                )
    pl.semaphore_wait(barrier, len(near) + T - 1)

    def send(src, dst, send_sem, recv_sem, dev):
        copy = pltpu.make_async_remote_copy(
            src_ref=src, dst_ref=dst, send_sem=send_sem, recv_sem=recv_sem,
            device_id=dev, device_id_type=MESH,
        )
        copy.start()
        return copy

    pending = []
    arrive_k, arrive_v = {}, {}

    def send_kv(src, i, dev, part):
        buf = (kbuf, vbuf)[part]
        copy = send(src, buf.at[i], kv_send.at[i, part], kv_recv.at[i, part], (dev, t))
        (arrive_k, arrive_v)[part][i] = copy
        pending.append(copy)

    for part, ref in ((0, k_ref), (1, v_ref)):
        send_kv(ref, 0, s_next, part)
        send_kv(ref, W - 1, z_next, part)

    arrive_w = {}
    order = [j for i in range(1, X // 2 + 1) for j in dict.fromkeys((i, X - i))]
    for j in [0] + order:
        for other in (0, 1):
            if j or other:
                dest = peer(j, other)
                cols = pl.ds(pl.multiple_of(dest * hd, hd), hd)
                copy = send(
                    w_ref.at[:, cols], wbuf.at[j, other],
                    w_send.at[j, other], w_recv.at[j, other], (s, dest),
                )
                arrive_w[j, other] = copy
                pending.append(copy)

    row = lax.broadcasted_iota(jnp.int32, (n, n), 0)
    col = lax.broadcasted_iota(jnp.int32, (n, n), 1)
    eye = row == col
    sizes = [CH]
    while sizes[-1] < n:
        sizes.append(sizes[-1] * 2)
    masks = [
        (row // a > col // a) & (row // (2 * a) == col // (2 * a)) for a in sizes[:-1]
    ]
    eta = rate_ref[0]

    def solve(k, v, rate):
        kf = k.astype(F32)
        r = 1.0 / jnp.sqrt(hd * (jnp.mean(kf * kf, axis=1, keepdims=True) + 1e-06))
        r_row = jnp.sum(jnp.where(eye, r, 0.0), axis=0, keepdims=True)
        low = mm_bt(k, k) * (rate * r) * r_row
        inv = jnp.where(masks[0], low, 0.0)
        for mask in masks[1:]:
            inv_b = inv.astype(BF16)
            step = jnp.where(mask, low, 0.0)
            step = step - mm(inv_b, step.astype(BF16))
            step = step - mm(step.astype(BF16), inv_b)
            inv = inv + step
        w_k = r * kf - mm((inv * r_row).astype(BF16), k)
        w_v = v.astype(F32) - mm(inv.astype(BF16), v)
        return r, r_row, w_k, w_v

    def block_map(k, v, rate):
        r, _, w_k, w_v = solve(k, v, rate)
        both = jnp.concatenate([w_k, w_v], axis=1) * (rate * r)
        return mm_at(k, both.astype(BF16))

    def compose(later, earlier, earlier_b):
        later_lin = later[:, :hd]
        flip = jnp.concatenate([earlier[:, :hd], earlier[:, hd:]], axis=1)
        return later + flip - mm(later_lin.astype(BF16), earlier_b)

    q, k_own, v_own = q_ref[...], k_ref[...], v_ref[...]
    qk = mm_bt(q, k_own)
    r, r_row, w_k, w_v = solve(k_own, v_own, eta)
    reads = jnp.where(row // CH > col // CH, qk * r_row * eta, 0.0).astype(BF16)
    read_lin = q.astype(F32) - mm(reads, w_k.astype(BF16))
    read_off = mm(reads, w_v.astype(BF16))

    newer = older = None
    for step in range(up):
        lo, hi = step, W - 1 - step
        for part, arrive in ((0, arrive_k), (1, arrive_v)):
            buf = (kbuf, vbuf)[part]
            arrive[lo].wait_recv()
            if step + 1 < up:
                send_kv(buf.at[lo], lo + 1, s_next, part)
            arrive[hi].wait_recv()
            if step + 1 < up:
                send_kv(buf.at[hi], hi - 1, s_prev, part)
        maps = []
        for i in (lo, hi):
            rate = jnp.where(s >= i + 1, eta, 0.0)
            maps.append(block_map(kbuf[i], vbuf[i], rate))
        if newer is None:
            newer, older = maps
        else:
            newer = compose(newer, maps[0], maps[0].astype(BF16))
            older = compose(maps[1], older, older.astype(BF16))
    total = compose(newer, older, older.astype(BF16))

    zbuf[0] = total.astype(BF16)
    arrive_z = {}

    def send_z(i, to, dev):
        copy = send(zbuf.at[i], zbuf.at[to], z_send.at[to], z_recv.at[to], (dev, t))
        arrive_z[to] = copy
        pending.append(copy)

    send_z(0, 1, z_next)
    if NZ - 1 > zup:
        send_z(0, NZ - 1, z_prev)

    scale = 1.0 / math.sqrt(hd)
    scores = [jnp.where(col <= row, qk * scale, -jnp.inf)]
    for i in range(W):
        part = mm_bt(q, kbuf[i]) * scale
        seen = s >= i + 1
        if i == W - 1:
            seen = seen & (col > row)
        scores.append(jnp.where(seen, part, -jnp.inf))
    top = functools.reduce(jnp.maximum, scores)
    top = jnp.max(top, axis=1, keepdims=True)
    expd = [jnp.exp(part - top) for part in scores]
    norm = 1.0 / jnp.sum(functools.reduce(jnp.add, expd), axis=1, keepdims=True)
    attended = mm((expd[0] * norm).astype(BF16), v_own)
    for i in range(W):
        attended = attended + mm((expd[i + 1] * norm).astype(BF16), vbuf[i])

    state = init_ref[0]
    for step in range(zup):
        lo, hi = step + 1, NZ - 1 - step
        arrive_z[lo].wait_recv()
        if lo < zup:
            send_z(lo, lo + 1, z_next)
        if hi > zup:
            arrive_z[hi].wait_recv()
            if hi - 1 > zup:
                send_z(hi, hi - 1, z_prev)
        for i in (lo, hi)[: 2 if hi > zup else 1]:
            got = jnp.where(z >= i, zbuf[i].astype(F32), 0.0)
            got_b = got.astype(BF16)
            if i == lo:
                total = compose(total, got, got_b)
            else:
                state = state + got[:, hd:] - mm(got_b[:, :hd], state.astype(BF16))
    state_b = state.astype(BF16)
    state = state + total[:, hd:] - mm(total[:, :hd].astype(BF16), state_b)

    state_b = state.astype(BF16)
    state_l = (state - state_b.astype(F32)).astype(BF16)
    lin_b = read_lin.astype(BF16)
    lin_l = (read_lin - lin_b.astype(F32)).astype(BF16)
    memory_read = mm(lin_b, state_b) + mm(lin_l, state_b) + mm(lin_b, state_l) + read_off
    gated = (attended * jax.nn.sigmoid(memory_read)).astype(BF16)
    gbuf[0, 0] = gated

    arrive_g = {}

    def send_g(j, to, dev):
        copy = send(gbuf.at[j, 0], gbuf.at[to], g_send.at[to], g_recv.at[to], (s, dev))
        arrive_g[to] = copy
        pending.append(copy)

    for j in order:
        send_g(0, (j, 0), peer(j, 0))
    send_g(0, (0, 1), partner)

    mine = w_ref[:, pl.ds(pl.multiple_of(t * hd, hd), hd)]
    out = mm(gated, mine)
    for copy in arrive_w.values():
        copy.wait_recv()
    for j in order:
        arrive_g[j, 0].wait_recv()
        send_g(j, (j, 1), partner)
        out = out + mm(gbuf[j, 0], wbuf[j, 0])
    for j in [0] + order:
        arrive_g[j, 1].wait_recv()
        out = out + mm(gbuf[j, 1], wbuf[j, 1])
    o_ref[...] = out.astype(o_ref.dtype)
    for copy in pending:
        copy.wait_send()


def solution(mesh):
    S, T = mesh.shape["seq"], mesh.shape["tp"]

    def step(queries, keys, values, step_rate, memory_init, out_weight):
        n, hd = queries.shape
        W = WIN // n
        X, NZ = T // 2, S // W
        vmem = pl.BlockSpec(memory_space=pltpu.VMEM)
        return pl.pallas_call(
            functools.partial(kernel, S, T, W),
            out_shape=jax.ShapeDtypeStruct((n, hd), jnp.bfloat16),
            in_specs=[pl.BlockSpec(memory_space=pltpu.SMEM)] + [vmem] * 5,
            out_specs=vmem,
            scratch_shapes=[
                pltpu.VMEM((W, n, hd), BF16),
                pltpu.VMEM((W, n, hd), BF16),
                pltpu.VMEM((NZ, hd, 2 * hd), BF16),
                pltpu.VMEM((X, 2, n, hd), BF16),
                pltpu.VMEM((X, 2, hd, hd), BF16),
                pltpu.SemaphoreType.DMA((W, 2)),
                pltpu.SemaphoreType.DMA((W, 2)),
                pltpu.SemaphoreType.DMA((NZ,)),
                pltpu.SemaphoreType.DMA((NZ,)),
                pltpu.SemaphoreType.DMA((X, 2)),
                pltpu.SemaphoreType.DMA((X, 2)),
                pltpu.SemaphoreType.DMA((X, 2)),
                pltpu.SemaphoreType.DMA((X, 2)),
            ],
            compiler_params=pltpu.CompilerParams(collective_id=0, has_side_effects=True),
        )(step_rate, queries, keys, values, memory_init, out_weight)

    return jax.shard_map(
        step,
        mesh=mesh,
        in_specs=(
            P("seq", "tp"),
            P("seq", "tp"),
            P("seq", "tp"),
            P("tp"),
            P("tp", None, None),
            P("tp", None),
        ),
        out_specs=P("seq", "tp"),
        check_vma=False,
    )
```

time: 432 us -> 65.9 us (0.15); the launches traced: 425 us -> 65.7 us
  waiting for transfers between devices: 220 us -> 0 us
  matrix products: 144 us -> 0 us
  Pallas kernels: 0 us -> 63.7 us
  starting transfers between devices: 35 us -> 0 us
  between operations: 14.4 us -> 0.66 us
    all_gather x2 -> x0, waiting for transfers between devices: 149 us -> none  [prefix(): everything = jax.tree.map(lambda part: lax.all_gather(part, axis), shard)]
    dot_general x145 -> x0, matrix products: 144 us -> none  [the longest x69 70.7 us: compose(): jnp.einsum('...ij,...jk->...ik', later[0], earlier[1], precision=highest)]
    pallas_call x0 -> x1, Pallas kernels: none -> 63.7 us  [step(): pl.pallas_call(functools.partial(kernel, S, T, W), out_shape=jax.ShapeDty...]
    unnamed x4 -> x0, waiting for transfers between devices: 61.1 us -> none
    ppermute x8 -> x0, starting transfers between devices: 34.9 us -> none  [shifted(): return lax.ppermute(block, axis, route)]
    ppermute x8 -> x0, waiting for transfers between devices: 10.3 us -> none  [shifted(): return lax.ppermute(block, axis, route)]
  transfers between devices with their start and end apart: 11 -> 0, of which waited for: 11 -> 0; matrix products, arithmetic and copies ran while one was open for 1% -> 0% of each run, Pallas kernels for 0% -> 0%
where the time goes in v1:
time: 65.9 us; the launch traced here: 65.7 us
  Pallas kernels  63.7 us (97%)
  local copies, waits for them, and re-layouts  1.38 us (2%)
  between operations  0.66 us (1%)
    pallas_call x1, Pallas kernels, step(): pl.pallas_call(functools.partial(kernel, S, T, W), out_shape=jax.ShapeDty...  63.7 us
    unnamed x1, local copies, waits for them, and re-layouts  1.38 us

profile of v1, /device:TPU:1, one launch (start us, length us, event | category | flops | bytes accessed | tf_op | source)
XLA Modules:
  0.0 65.7 jit_solution(16224881189326536195)
XLA Ops:
  0.7 63.7 %shard_map.64 = bf16[128,128]{1,0:T(8,128)(2,1)} custom-call(f32[1]{0:T(128)S(6)} %copy.8.rate_ref, bf16[128,128]{1,0:T(8,128)(2,1)} %q_ref.1, bf16[128,128]{1,0:T(8,128)(2,1)} %k_ref.1, bf16[128,128]{1,0:T(8,128)(2,1)} %v_ref.1, f32[1,128,128]{2,1,0:T(8,128)} %init_ref.1, bf16[128,2048]{1,0:T(8,128)(2,1)} %w_ref.1), custom_call_target="tpu_custom_call" | custom-call | tf_op jit(solution)/shard_map/pallas_call | solution.py:254
  64.3 1.4 %copy.9 = bf16[128,128]{1,0:T(8,128)(2,1)} copy(bf16[128,128]{1,0:T(8,128)(2,1)} %shard_map.64) | data formatting | bytes 65536

commit v2 on v1

v2 whole, which is shorter than its diff:
```python
import functools
import math

import jax
import jax.numpy as jnp
from jax import lax
from jax.experimental import pallas as pl
from jax.experimental.pallas import tpu as pltpu
from jax.sharding import PartitionSpec as P

WIN = 1024
CH = 16
MESH = pl.DeviceIdType.MESH
F32 = jnp.float32
BF16 = jnp.bfloat16


def mm(a, b):
    return lax.dot_general(a, b, (((1,), (0,)), ((), ())), preferred_element_type=F32)


def mm_bt(a, b):
    return lax.dot_general(a, b, (((1,), (1,)), ((), ())), preferred_element_type=F32)


def mm_at(a, b):
    return lax.dot_general(a, b, (((0,), (0,)), ((), ())), preferred_element_type=F32)


def kernel(
    S, T, W,
    rate_ref, q_hbm, k_hbm, v_hbm, init_hbm, w_hbm, o_ref,
    q_ref, k_ref, v_ref, state_ref, own_w, kbuf, vbuf, map_out, map_in, m_out, m_in,
    gbuf, wbuf,
    in_sem, ready, kv_send, kv_recv, m_send, m_recv, g_send, g_recv, w_send, w_recv,
):
    n, hd = q_ref.shape
    X, half = T // 2, W // 2
    s, t = lax.axis_index("seq"), lax.axis_index("tp")
    x, core = t // 2, lax.rem(t, 2)
    z, y = s // W, lax.rem(s, W)
    partner = x * 2 + 1 - core

    def peer(j, other):
        xj = lax.rem(x + j, X)
        return xj * 2 + (1 - core if other else core)

    def cols(dest):
        return pl.ds(pl.multiple_of(dest * hd, hd), hd)

    def signal(sem, dev):
        pl.semaphore_signal(sem, inc=1, device_id=dev, device_id_type=MESH)

    barrier = pltpu.get_barrier_semaphore()
    wrap = range(half + 1, W)
    cross = [d for i in range(1, half + 1) for d in dict.fromkeys((i, W - i))]
    row_links = [(1, y + 1 < W), (-1, y >= 1)]
    row_links += [(d, y + d < W) for d in wrap] + [(-d, y >= d) for d in wrap]
    next_links = [(W, s + W < S), (2 * W, s + 2 * W < S)]
    next_links += [(d, (y + d >= W) & (s + d < S)) for d in cross]
    for d, there in row_links + next_links:

        @pl.when(there)
        def _():
            signal(barrier, (s + d, t))

    for j in range(X):
        for other in (0, 1):
            if j or other:
                signal(barrier, (s, peer(j, other)))

    loads = [
        pltpu.make_async_copy(src, dst, in_sem.at[i])
        for i, (src, dst) in enumerate(
            (
                (k_hbm, k_ref),
                (v_hbm, v_ref),
                (q_hbm, q_ref),
                (init_hbm.at[0], state_ref),
                (w_hbm.at[:, cols(t)], own_w),
            )
        )
    ]
    for load in loads:
        load.start()

    for yy in range(W):
        in_row = (yy + 1 < W) + (yy >= 1)
        in_row += sum((yy + d < W) + (yy >= d) for d in wrap)
        earlier = 1 + sum(yy < d for d in cross)
        for zz, more in enumerate((0, earlier, earlier + 1)):

            @pl.when((y == yy) & (z == zz if zz < 2 else z >= 2))
            def _():
                pl.semaphore_wait(barrier, T - 1 + in_row + more)

    @pl.when(z >= 1)
    def _():
        signal(ready.at[0], (s - W, t))

    @pl.when(z >= 2)
    def _():
        signal(ready.at[W], (s - 2 * W, t))

    for d in cross:

        @pl.when((y < d) & (z >= 1))
        def _():
            signal(ready.at[d], (s - d, t))

    def copy_to(src, dst, send_sem, recv_sem, dev):
        return pltpu.make_async_remote_copy(
            src_ref=src, dst_ref=dst, send_sem=send_sem, recv_sem=recv_sem,
            device_id=dev, device_id_type=MESH,
        )

    sent = []

    def kv_send_to(src, d, part, dev, there):
        i = sum(p == part for p, _, _ in sent)
        dst = (kbuf, vbuf)[part].at[d - 1]

        def make():
            return copy_to(src, dst, kv_send.at[i, part], kv_recv.at[d - 1, part], (dev, t))

        @pl.when(there)
        def _():
            make().start()

        sent.append((part, make, there))

    def kv_arrive(d, part):
        buf = (kbuf, vbuf)[part].at[d - 1]
        return copy_to(
            buf, buf, kv_send.at[0, part], kv_recv.at[d - 1, part], (lax.rem(s + 1, S), t)
        )

    for part, src in ((0, k_hbm), (1, v_hbm)):
        kv_send_to(src, 1, part, s + 1, y + 1 < W)
    for d in wrap:
        for part, src in ((0, k_hbm), (1, v_hbm)):
            kv_send_to(src, d, part, s + d, y + d < W)

    order = [j for i in range(1, X // 2 + 1) for j in dict.fromkeys((i, X - i))]
    w_copies, g_copies = {}, {}
    for j in [0] + order:
        for other in (0, 1):
            if j or other:
                dest = peer(j, other)
                copy = copy_to(
                    w_hbm.at[:, cols(dest)], wbuf.at[j, other],
                    w_send.at[j, other], w_recv.at[j, other], (s, dest),
                )
                copy.start()
                w_copies[j, other] = copy

    row = lax.broadcasted_iota(jnp.int32, (n, n), 0)
    col = lax.broadcasted_iota(jnp.int32, (n, n), 1)
    eye = row == col
    sizes = [CH]
    while sizes[-1] < n:
        sizes.append(sizes[-1] * 2)
    masks = [
        (row // a > col // a) & (row // (2 * a) == col // (2 * a)) for a in sizes[:-1]
    ]
    eta = rate_ref[0]

    def solve(k, v, rate):
        kf = k.astype(F32)
        r = 1.0 / jnp.sqrt(hd * (jnp.mean(kf * kf, axis=1, keepdims=True) + 1e-06))
        r_row = jnp.sum(jnp.where(eye, r, 0.0), axis=0, keepdims=True)
        low = mm_bt(k, k) * (rate * r) * r_row
        inv = jnp.where(masks[0], low, 0.0)
        for mask in masks[1:]:
            inv_b = inv.astype(BF16)
            step = jnp.where(mask, low, 0.0)
            step = step - mm(inv_b, step.astype(BF16))
            step = step - mm(step.astype(BF16), inv_b)
            inv = inv + step
        w_k = r * kf - mm((inv * r_row).astype(BF16), k)
        w_v = v.astype(F32) - mm(inv.astype(BF16), v)
        return r, r_row, w_k, w_v

    def block_map(k, v, rate):
        r, _, w_k, w_v = solve(k, v, rate)
        both = jnp.concatenate([w_k, w_v], axis=1) * (rate * r)
        return mm_at(k, both.astype(BF16))

    def compose(later, earlier, earlier_b):
        later_lin = later[:, :hd]
        flip = jnp.concatenate([earlier[:, :hd], earlier[:, hd:]], axis=1)
        return later + flip - mm(later_lin.astype(BF16), earlier_b)

    for load in loads:
        load.wait()
    q, k_own, v_own = q_ref[...], k_ref[...], v_ref[...]
    qk = mm_bt(q, k_own)
    r, r_row, w_k, w_v = solve(k_own, v_own, eta)
    reads = jnp.where(row // CH > col // CH, qk * r_row * eta, 0.0).astype(BF16)
    read_lin = q.astype(F32) - mm(reads, w_k.astype(BF16))
    read_off = mm(reads, w_v.astype(BF16))

    @pl.when(s + W < S)
    def _():
        pl.semaphore_wait(ready.at[0], 1)

    for part, src in ((0, k_hbm), (1, v_hbm)):
        kv_send_to(src, W, part, s + W, s + W < S)
    for d in cross:
        there = (y + d >= W) & (s + d < S)

        @pl.when(there)
        def _():
            pl.semaphore_wait(ready.at[d], 1)

        for part, src in ((0, k_hbm), (1, v_hbm)):
            kv_send_to(src, d, part, s + d, there)

    newer = older = None
    for step in range(half):
        lo, hi = step + 1, W - step
        for part, buf in ((0, kbuf), (1, vbuf)):
            for d in (lo, hi):

                @pl.when(s >= d)
                def _():
                    kv_arrive(d, part).wait_recv()

                @pl.when(s < d)
                def _():
                    buf[d - 1] = jnp.zeros((n, hd), BF16)

                src = buf.at[d - 1]
                if d == lo and lo < half:
                    kv_send_to(src, d + 1, part, s + 1, (y >= d) & (y + 1 < W))
        maps = [block_map(kbuf[d - 1], vbuf[d - 1], eta) for d in (lo, hi)]
        if newer is None:
            newer, older = maps
        else:
            newer = compose(newer, maps[0], maps[0].astype(BF16))
            older = compose(maps[1], older, older.astype(BF16))
    total = compose(newer, older, older.astype(BF16))

    def map_copy():
        return copy_to(map_out, map_in, m_send.at[0], m_recv.at[0], (lax.rem(s + W, S), t))

    def m_copy():
        return copy_to(m_out, m_in, m_send.at[1], m_recv.at[1], (lax.rem(s + 2 * W, S), t))

    map_out[...] = total.astype(BF16)

    @pl.when(s + W < S)
    def _():
        map_copy().start()

    scale = 1.0 / math.sqrt(hd)
    scores = [jnp.where(col <= row, qk * scale, -jnp.inf)]
    for i in range(W):
        part = mm_bt(q, kbuf[i]) * scale
        seen = s >= i + 1
        if i == W - 1:
            seen = seen & (col > row)
        scores.append(jnp.where(seen, part, -jnp.inf))
    top = functools.reduce(jnp.maximum, scores)
    top = jnp.max(top, axis=1, keepdims=True)
    expd = [jnp.exp(part - top) for part in scores]
    norm = 1.0 / jnp.sum(functools.reduce(jnp.add, expd), axis=1, keepdims=True)
    attended = mm((expd[0] * norm).astype(BF16), v_own)
    for i in range(W):
        attended = attended + mm((expd[i + 1] * norm).astype(BF16), vbuf[i])

    @pl.when(z >= 1)
    def _():
        map_copy().wait_recv()

    @pl.when(z < 1)
    def _():
        map_in[...] = jnp.zeros((hd, 2 * hd), BF16)

    before = map_in[...]
    total = compose(total, before.astype(F32), before)

    @pl.when(z >= 2)
    def _():
        m_copy().wait_recv()
        state_ref[...] = m_in[...].astype(F32)

    state = state_ref[...]
    state = state + total[:, hd:] - mm(total[:, :hd].astype(BF16), state.astype(BF16))
    state_b = state.astype(BF16)
    m_out[...] = state_b

    @pl.when(s + 2 * W < S)
    def _():
        pl.semaphore_wait(ready.at[W], 1)
        m_copy().start()

    state_l = (state - state_b.astype(F32)).astype(BF16)
    lin_b = read_lin.astype(BF16)
    lin_l = (read_lin - lin_b.astype(F32)).astype(BF16)
    memory_read = mm(lin_b, state_b) + mm(lin_l, state_b) + mm(lin_b, state_l) + read_off
    gated = (attended * jax.nn.sigmoid(memory_read)).astype(BF16)
    gbuf[0, 0] = gated

    def send_g(j, to, dev):
        copy = copy_to(gbuf.at[j, 0], gbuf.at[to], g_send.at[to], g_recv.at[to], (s, dev))
        copy.start()
        g_copies[to] = copy

    for j in order:
        send_g(0, (j, 0), peer(j, 0))
    send_g(0, (0, 1), partner)

    out = mm(gated, own_w[...])
    for copy in w_copies.values():
        copy.wait_recv()
    for j in order:
        g_copies[j, 0].wait_recv()
        send_g(j, (j, 1), partner)
        out = out + mm(gbuf[j, 0], wbuf[j, 0])
    for j in [0] + order:
        g_copies[j, 1].wait_recv()
        out = out + mm(gbuf[j, 1], wbuf[j, 1])
    o_ref[...] = out.astype(o_ref.dtype)

    for _, make, there in sent:

        @pl.when(there)
        def _():
            make().wait_send()

    @pl.when(s + W < S)
    def _():
        map_copy().wait_send()

    @pl.when(s + 2 * W < S)
    def _():
        m_copy().wait_send()

    for copy in [*w_copies.values(), *g_copies.values()]:
        copy.wait_send()


def solution(mesh):
    S, T = mesh.shape["seq"], mesh.shape["tp"]

    def step(queries, keys, values, step_rate, memory_init, out_weight):
        n, hd = queries.shape
        W = WIN // n
        X = T // 2
        dma = pltpu.SemaphoreType.DMA
        anywhere = pl.BlockSpec(memory_space=pl.ANY)
        return pl.pallas_call(
            functools.partial(kernel, S, T, W),
            out_shape=jax.ShapeDtypeStruct((n, hd), jnp.bfloat16),
            in_specs=[pl.BlockSpec(memory_space=pltpu.SMEM)] + [anywhere] * 5,
            out_specs=pl.BlockSpec(memory_space=pltpu.VMEM),
            scratch_shapes=[
                pltpu.VMEM((n, hd), BF16),
                pltpu.VMEM((n, hd), BF16),
                pltpu.VMEM((n, hd), BF16),
                pltpu.VMEM((hd, hd), F32),
                pltpu.VMEM((hd, hd), BF16),
                pltpu.VMEM((W, n, hd), BF16),
                pltpu.VMEM((W, n, hd), BF16),
                pltpu.VMEM((hd, 2 * hd), BF16),
                pltpu.VMEM((hd, 2 * hd), BF16),
                pltpu.VMEM((hd, hd), BF16),
                pltpu.VMEM((hd, hd), BF16),
                pltpu.VMEM((X, 2, n, hd), BF16),
                pltpu.VMEM((X, 2, hd, hd), BF16),
                dma((5,)),
                pltpu.SemaphoreType.REGULAR((W + 1,)),
                dma((3 * W, 2)),
                dma((W, 2)),
                dma((2,)),
                dma((2,)),
                dma((X, 2)),
                dma((X, 2)),
                dma((X, 2)),
                dma((X, 2)),
            ],
            compiler_params=pltpu.CompilerParams(collective_id=0, has_side_effects=True),
        )(step_rate, queries, keys, values, memory_init, out_weight)

    return jax.shard_map(
        step,
        mesh=mesh,
        in_specs=(
            P("seq", "tp"),
            P("seq", "tp"),
            P("seq", "tp"),
            P("tp"),
            P("tp", None, None),
            P("tp", None),
        ),
        out_specs=P("seq", "tp"),
        check_vma=False,
    )
```

time: 65.9 us -> 48.4 us (0.73)
  the two profiles are of different devices: /device:TPU:1 before, /device:TPU:897 now
where the time goes in v2:
time: 48.4 us; the launch traced here: 48.2 us
  Pallas kernels  46.1 us (95%)
  local copies, waits for them, and re-layouts  1.38 us (3%)
  between operations  0.66 us (1%)
    pallas_call x1, Pallas kernels, step(): pl.pallas_call(functools.partial(kernel, S, T, W), out_shape=jax.ShapeDty...  46.1 us
    unnamed x1, local copies, waits for them, and re-layouts  1.38 us

profile of v2, /device:TPU:897, one launch (start us, length us, event | category | flops | bytes accessed | tf_op | source)
XLA Modules:
  0.0 48.2 jit_solution(5250851094759037248)
XLA Ops:
  0.7 46.1 %shard_map.64 = bf16[128,128]{1,0:T(8,128)(2,1)} custom-call(f32[1]{0:T(128)S(6)} %copy.8.rate_ref, bf16[128,128]{1,0:T(8,128)(2,1)} %q_hbm.1, bf16[128,128]{1,0:T(8,128)(2,1)} %k_hbm.1, bf16[128,128]{1,0:T(8,128)(2,1)} %v_hbm.1, f32[1,128,128]{2,1,0:T(8,128)} %init_hbm.1, bf16[128,2048]{1,0:T(8,128)(2,1)} %w_hbm.1), custom_call_target="tpu_custom_call" | custom-call | tf_op jit(solution)/shard_map/pallas_call | solution.py:353
  46.8 1.4 %copy.9 = bf16[128,128]{1,0:T(8,128)(2,1)} copy(bf16[128,128]{1,0:T(8,128)(2,1)} %shard_map.64) | data formatting | bytes 65536

commit v3 on v2

--- a/solution.py
+++ b/solution.py
@@ -31,7 +31,7 @@
     S, T, W,
     rate_ref, q_hbm, k_hbm, v_hbm, init_hbm, w_hbm, o_ref,
     q_ref, k_ref, v_ref, state_ref, own_w, kbuf, vbuf, map_out, map_in, m_out, m_in,
-    gbuf, wbuf,
+    near_ref, far_ref, gbuf, wbuf,
     in_sem, ready, kv_send, kv_recv, m_send, m_recv, g_send, g_recv, w_send, w_recv,
 ):
     n, hd = q_ref.shape
@@ -52,10 +52,10 @@
         pl.semaphore_signal(sem, inc=1, device_id=dev, device_id_type=MESH)
 
     barrier = pltpu.get_barrier_semaphore()
-    wrap = range(half + 1, W)
-    cross = [d for i in range(1, half + 1) for d in dict.fromkeys((i, W - i))]
-    row_links = [(1, y + 1 < W), (-1, y >= 1)]
-    row_links += [(d, y + d < W) for d in wrap] + [(-d, y >= d) for d in wrap]
+    reach = min(half, 2)
+    direct = [*range(1, reach + 1), *range(half + 1, W)]
+    cross = range(1, W)
+    row_links = [(d, y + d < W) for d in direct] + [(-d, y >= d) for d in direct]
     next_links = [(W, s + W < S), (2 * W, s + 2 * W < S)]
     next_links += [(d, (y + d >= W) & (s + d < S)) for d in cross]
     for d, there in row_links + next_links:
@@ -85,8 +85,7 @@
         load.start()
 
     for yy in range(W):
-        in_row = (yy + 1 < W) + (yy >= 1)
-        in_row += sum((yy + d < W) + (yy >= d) for d in wrap)
+        in_row = sum((yy + d < W) + (yy >= d) for d in direct)
         earlier = 1 + sum(yy < d for d in cross)
         for zz, more in enumerate((0, earlier, earlier + 1)):
 
@@ -135,9 +134,7 @@
             buf, buf, kv_send.at[0, part], kv_recv.at[d - 1, part], (lax.rem(s + 1, S), t)
         )
 
-    for part, src in ((0, k_hbm), (1, v_hbm)):
-        kv_send_to(src, 1, part, s + 1, y + 1 < W)
-    for d in wrap:
+    for d in direct:
         for part, src in ((0, k_hbm), (1, v_hbm)):
             kv_send_to(src, d, part, s + d, y + d < W)
 
@@ -191,6 +188,17 @@
         flip = jnp.concatenate([earlier[:, :hd], earlier[:, hd:]], axis=1)
         return later + flip - mm(later_lin.astype(BF16), earlier_b)
 
+    def send_later(now):
+        for d in range(1, W + 1):
+            there = (y + d >= W) & (s + d < S) & now(d)
+
+            @pl.when(there)
+            def _():
+                pl.semaphore_wait(ready.at[d % W], 1)
+
+            for part, src in ((0, k_hbm), (1, v_hbm)):
+                kv_send_to(src, d, part, s + d, there)
+
     for load in loads:
         load.wait()
     q, k_own, v_own = q_ref[...], k_ref[...], v_ref[...]
@@ -200,46 +208,72 @@
     read_lin = q.astype(F32) - mm(reads, w_k.astype(BF16))
     read_off = mm(reads, w_v.astype(BF16))
 
-    @pl.when(s + W < S)
-    def _():
-        pl.semaphore_wait(ready.at[0], 1)
-
-    for part, src in ((0, k_hbm), (1, v_hbm)):
-        kv_send_to(src, W, part, s + W, s + W < S)
-    for d in cross:
-        there = (y + d >= W) & (s + d < S)
-
-        @pl.when(there)
-        def _():
-            pl.semaphore_wait(ready.at[d], 1)
-
-        for part, src in ((0, k_hbm), (1, v_hbm)):
-            kv_send_to(src, d, part, s + d, there)
-
-    newer = older = None
-    for step in range(half):
-        lo, hi = step + 1, W - step
+    send_later(lambda d: (y + d < W + half) & (d <= half))
+    if half > reach:
         for part, buf in ((0, kbuf), (1, vbuf)):
-            for d in (lo, hi):
-
-                @pl.when(s >= d)
-                def _():
-                    kv_arrive(d, part).wait_recv()
-
-                @pl.when(s < d)
-                def _():
-                    buf[d - 1] = jnp.zeros((n, hd), BF16)
-
-                src = buf.at[d - 1]
-                if d == lo and lo < half:
-                    kv_send_to(src, d + 1, part, s + 1, (y >= d) & (y + 1 < W))
-        maps = [block_map(kbuf[d - 1], vbuf[d - 1], eta) for d in (lo, hi)]
-        if newer is None:
-            newer, older = maps
-        else:
-            newer = compose(newer, maps[0], maps[0].astype(BF16))
-            older = compose(maps[1], older, older.astype(BF16))
-    total = compose(newer, older, older.astype(BF16))
+
+            @pl.when((y >= reach) & (y + 1 < W))
+            def _():
+                kv_arrive(reach, part).wait_recv()
+
+            for d in range(reach + 1, half + 1):
+                hop = d - reach
+                there = (y >= reach) & (y + hop < W)
+                kv_send_to(buf.at[reach - 1], d, part, s + hop, there)
+    send_later(lambda d: d > half)
+
+    def maps_of(distances):
+        return [block_map(kbuf[d - 1], vbuf[d - 1], eta) for d in distances]
+
+    def join(maps):
+        return functools.reduce(lambda p, m: compose(p, m, m.astype(BF16)), maps)
+
+    full = (z >= 1) | (y > half)
+    for first in range(half):
+        steps = range(first, first + 1)
+        near, far = [i + 1 for i in steps], [W - i for i in steps][::-1]
+        for step in steps:
+            lo, hi = step + 1, W - step
+            for part, buf in ((0, kbuf), (1, vbuf)):
+                for d in (lo, hi):
+
+                    @pl.when((s >= d) & ((y < d) | (y + 1 >= W)) if d == reach < half else s >= d)
+                    def _():
+                        kv_arrive(d, part).wait_recv()
+
+                    @pl.when(s < d)
+                    def _():
+                        buf[d - 1] = jnp.zeros((n, hd), BF16)
+
+        @pl.when(full)
+        def _():
+            maps = maps_of(near + far)
+            newer, older = join(maps[: len(near)]), join(maps[len(near) :])
+            if first:
+                newer = compose(near_ref[...], newer, newer.astype(BF16))
+                earlier = far_ref[...]
+                older = compose(older, earlier, earlier.astype(BF16))
+            near_ref[...] = newer
+            far_ref[...] = older
+
+        @pl.when((z == 0) & (y <= half) & (y >= near[0]))
+        def _():
+            newer = join(maps_of(near))
+            if first:
+                newer = compose(near_ref[...], newer, newer.astype(BF16))
+            else:
+                far_ref[...] = jnp.zeros((hd, 2 * hd), F32)
+            near_ref[...] = newer
+
+        if not first:
+
+            @pl.when(s == 0)
+            def _():
+                near_ref[...] = jnp.zeros((hd, 2 * hd), F32)
+                far_ref[...] = jnp.zeros((hd, 2 * hd), F32)
+
+    older = far_ref[...]
+    total = compose(near_ref[...], older, older.astype(BF16))
 
     def map_copy():
         return copy_to(map_out, map_in, m_send.at[0], m_recv.at[0], (lax.rem(s + W, S), t))
@@ -367,6 +401,8 @@
                 pltpu.VMEM((hd, 2 * hd), BF16),
                 pltpu.VMEM((hd, hd), BF16),
                 pltpu.VMEM((hd, hd), BF16),
+                pltpu.VMEM((hd, 2 * hd), F32),
+                pltpu.VMEM((hd, 2 * hd), F32),
                 pltpu.VMEM((X, 2, n, hd), BF16),
                 pltpu.VMEM((X, 2, hd, hd), BF16),
                 dma((5,)),

time: 48.4 us -> 47.7 us (0.986)
  Pallas kernels: 46.1 us -> 45.1 us
    pallas_call x1, Pallas kernels: 46.1 us -> 45.1 us  [step(): pl.pallas_call(functools.partial(kernel, S, T, W), out_shape=jax.ShapeDty...]
where the time goes in v3:
time: 47.7 us; the launch traced here: 47.2 us
  Pallas kernels  45.1 us (95%)
  local copies, waits for them, and re-layouts  1.38 us (3%)
  between operations  0.66 us (1%)
    pallas_call x1, Pallas kernels, step(): pl.pallas_call(functools.partial(kernel, S, T, W), out_shape=jax.ShapeDty...  45.1 us
    unnamed x1, local copies, waits for them, and re-layouts  1.38 us

profile of v3, /device:TPU:897, one launch (start us, length us, event | category | flops | bytes accessed | tf_op | source)
XLA Modules:
  0.0 47.2 jit_solution(7844027807221263240)
XLA Ops:
  0.7 45.1 %shard_map.64 = bf16[128,128]{1,0:T(8,128)(2,1)} custom-call(f32[1]{0:T(128)S(6)} %copy.8.rate_ref, bf16[128,128]{1,0:T(8,128)(2,1)} %q_hbm.1, bf16[128,128]{1,0:T(8,128)(2,1)} %k_hbm.1, bf16[128,128]{1,0:T(8,128)(2,1)} %v_hbm.1, f32[1,128,128]{2,1,0:T(8,128)} %init_hbm.1, bf16[128,2048]{1,0:T(8,128)(2,1)} %w_hbm.1), custom_call_target="tpu_custom_call" | custom-call | tf_op jit(solution)/shard_map/pallas_call | solution.py:387
  45.8 1.4 %copy.9 = bf16[128,128]{1,0:T(8,128)(2,1)} copy(bf16[128,128]{1,0:T(8,128)(2,1)} %shard_map.64) | data formatting | bytes 65536

commit v4 on v3

--- a/solution.py
+++ b/solution.py
@@ -231,9 +231,9 @@
     full = (z >= 1) | (y > half)
     for first in range(half):
         steps = range(first, first + 1)
-        near, far = [i + 1 for i in steps], [W - i for i in steps][::-1]
+        near, far = [i + 1 for i in steps], [half + 1 + i for i in steps]
         for step in steps:
-            lo, hi = step + 1, W - step
+            lo, hi = step + 1, half + 1 + step
             for part, buf in ((0, kbuf), (1, vbuf)):
                 for d in (lo, hi):
 
@@ -251,8 +251,7 @@
             newer, older = join(maps[: len(near)]), join(maps[len(near) :])
             if first:
                 newer = compose(near_ref[...], newer, newer.astype(BF16))
-                earlier = far_ref[...]
-                older = compose(older, earlier, earlier.astype(BF16))
+                older = compose(far_ref[...], older, older.astype(BF16))
             near_ref[...] = newer
             far_ref[...] = older
 

time: 47.7 us -> 47.9 us (level)
  no operation moved by 1% of the time
where the time goes in v4:
time: 47.9 us; the launch traced here: 47.2 us
  Pallas kernels  45.2 us (94%)
  local copies, waits for them, and re-layouts  1.38 us (3%)
  between operations  0.66 us (1%)
    pallas_call x1, Pallas kernels, step(): pl.pallas_call(functools.partial(kernel, S, T, W), out_shape=jax.ShapeDty...  45.2 us
    unnamed x1, local copies, waits for them, and re-layouts  1.38 us

profile of v4, /device:TPU:897, one launch (start us, length us, event | category | flops | bytes accessed | tf_op | source)
XLA Modules:
  0.0 47.2 jit_solution(8867232142211953371)
XLA Ops:
  0.7 45.2 %shard_map.64 = bf16[128,128]{1,0:T(8,128)(2,1)} custom-call(f32[1]{0:T(128)S(6)} %copy.8.rate_ref, bf16[128,128]{1,0:T(8,128)(2,1)} %q_hbm.1, bf16[128,128]{1,0:T(8,128)(2,1)} %k_hbm.1, bf16[128,128]{1,0:T(8,128)(2,1)} %v_hbm.1, f32[1,128,128]{2,1,0:T(8,128)} %init_hbm.1, bf16[128,2048]{1,0:T(8,128)(2,1)} %w_hbm.1), custom_call_target="tpu_custom_call" | custom-call | tf_op jit(solution)/shard_map/pallas_call | solution.py:386
  45.9 1.4 %copy.9 = bf16[128,128]{1,0:T(8,128)(2,1)} copy(bf16[128,128]{1,0:T(8,128)(2,1)} %shard_map.64) | data formatting | bytes 65536
